TPU v7x, 32 devices: a whole 2x2x4 slice. The times are simulated.
32 devices in a mesh: member: 2 (over x), gx: 16 (over z, y, core).
Axes of the slice: x: 2, y: 2, z: 4, core: 2. Of those that a mesh axis runs over, the one named last changes fastest.
Arguments:
- electric: float32 [3, 64, 256, 128], P(None, 'gx'), may hold values from -6 to 6
- magnetic: float32 [3, 64, 256, 128], P(None, 'gx'), may hold values from -6 to 6
- material: int32 [128, 256, 128], P(('member', 'gx')), parts along dimension 0, may hold values from 0 to 3, as said below
- permittivity: float32 [4], replicated, may hold values from 1 to 4
- pole_frequency: float32 [2], replicated, may hold values from 0.3 to 1.2
- pole_damping: float32 [2], replicated, may hold values from 0.05 to 1
- pole_strength: float32 [2], replicated, may hold values from 0.3 to 2
- frequencies: float32 [8], replicated, may hold values from 0.2 to 2
- plane_depth: int32 [4], replicated, may hold values from 1 to 126
- mode_fields: float32 [4, 4, 64, 256], P(None, None, 'gx'), may hold values from -40 to 40
Outputs:
- electric_final: float32 [3, 128, 256, 128], P(None, ('member', 'gx')), parts along dimension 1
- magnetic_final: float32 [3, 128, 256, 128], P(None, ('member', 'gx')), parts along dimension 1
- monitors: float32 [2, 4, 8, 4, 128, 256], P(None, None, None, None, ('member', 'gx')), parts along dimension 4
- intersection: float32 [4, 4, 8], P('member'), parts along dimension 0
There are 2 independent parts, one for each index of `member`. A program takes and returns all parts, laid end to end along the dimension named above; an argument that names none is the same for every part. Nothing has to cross between parts.
Inputs may be any that keep to these rules, and one draw needn't show every extreme that they name: Each 16-layer thickness profile stacks layers along the first dimension, each of one material, with a lateral lattice of material 0 cells in some layers; materials 2 and above are dispersive.
All inputs are finite; a program needn't handle non-finite values.
Results may differ from a plain program's by a relative error of at most 0.0003.
Values sent between devices are 32-bit elements; how exact they have to be, the bound alone decides.
A program may use at most 64 MiB of HBM per device.

v0:
```python
import functools
import math

import jax
import jax.numpy as jnp
from jax import lax
from jax.experimental import pallas as pl
from jax.experimental.pallas import tpu as pltpu
from jax.sharding import PartitionSpec as P

STEPS = 6
DT = 0.5
CHUNKS = 8
ROWS = 32
PAD = 8
MESH = pl.DeviceIdType.MESH
VMEM_BYTES = 67043328
F32 = jnp.float32
BF16 = jnp.bfloat16


def ahead(value):
    width = value.shape[-1]
    lane = lax.broadcasted_iota(jnp.int32, value.shape, 1)
    return jnp.where(lane == width - 1, 0.0, pltpu.roll(value, width - 1, 1))


def behind(value):
    lane = lax.broadcasted_iota(jnp.int32, value.shape, 1)
    return jnp.where(lane == 0, 0.0, pltpu.roll(value, 1, 1))


def main_kernel(
    count,
    scale,
    perm_ref,
    freq_ref,
    damp_ref,
    strength_ref,
    omega_ref,
    depth_ref,
    mode_ref,
    el_ref,
    ma_ref,
    mat_ref,
    eb,
    hb,
    mon_ref,
    inter_ref,
    ge,
    gh,
    jb,
    pb,
    coef,
    matb,
    planes,
    pick,
    part,
    gathered,
    rot,
    rot_s,
    in_sem,
    rot_sem,
    se_sem,
    re_sem,
    sh_sem,
    rh_sem,
    sp_sem,
    rp_sem,
):
    me = lax.axis_index("gx")
    layers, width, deep = mat_ref.shape
    nm, nf = depth_ref.shape[0], omega_ref.shape[0]
    chunk = width // CHUNKS
    has_upper = me < count - 1
    has_lower = me > 0
    top = layers - 1

    barrier = pltpu.get_barrier_semaphore()
    for k in range(1, count):
        pl.semaphore_signal(
            barrier, inc=1, device_id={"gx": lax.rem(me + k, count)}, device_id_type=MESH
        )

    loads = [
        pltpu.make_async_copy(el_ref, eb.at[:, :, pl.ds(0, width)], in_sem.at[0]),
        pltpu.make_async_copy(ma_ref, hb.at[:, :, pl.ds(PAD, width)], in_sem.at[1]),
        pltpu.make_async_copy(mat_ref, matb, in_sem.at[2]),
    ]
    for load in loads:
        load.start()

    def send_e(c, source):
        rows = pl.ds(c * chunk, chunk)
        return pltpu.make_async_remote_copy(
            src_ref=source.at[pl.ds(1, 2), 0, rows],
            dst_ref=ge.at[:, rows],
            send_sem=se_sem.at[c],
            recv_sem=re_sem.at[c],
            device_id={"gx": me - 1},
            device_id_type=MESH,
        )

    def send_h(c):
        return pltpu.make_async_remote_copy(
            src_ref=hb.at[pl.ds(1, 2), top, pl.ds(PAD + c * chunk, chunk)],
            dst_ref=gh.at[:, pl.ds(c * chunk, chunk)],
            send_sem=sh_sem.at[c],
            recv_sem=rh_sem.at[c],
            device_id={"gx": me + 1},
            device_id_type=MESH,
        )

    shape = pick.shape
    row = lax.broadcasted_iota(jnp.int32, shape, 0)
    col = lax.broadcasted_iota(jnp.int32, shape, 1)
    wanted = jnp.zeros(shape, jnp.int32)
    for m in range(nm):
        wanted = jnp.where(row // 8 == m, depth_ref[m], wanted)
    hit = (row % 8 == col // (2 * deep)) & (col % deep == wanted)
    pick[...] = jnp.where(hit, 1.0, 0.0).astype(BF16)

    lane = lax.broadcasted_iota(jnp.int32, (nf, deep), 1)
    line = lax.broadcasted_iota(jnp.int32, (nf, deep), 0)
    omega = jnp.zeros((nf, deep), F32)
    for f in range(nf):
        omega = jnp.where(line == f, omega_ref[f], omega)
    late = jnp.where(lane % 4 < 2, 1.0, 0.5)
    phase = ((lane // 4).astype(F32) + late) * DT * omega
    rot[0] = jnp.where(lane < 4 * STEPS, jnp.cos(phase), 0.0)
    rot[1] = jnp.where(lane < 4 * STEPS, -jnp.sin(phase), 0.0)

    zero_rows = jnp.zeros((PAD, deep), F32)
    for c in range(3):
        for x in range(layers):
            eb[c, x, pl.ds(width, PAD), :] = zero_rows
            hb[c, x, pl.ds(0, PAD), :] = zero_rows
    part[...] = jnp.zeros_like(part)

    pl.semaphore_wait(barrier, count - 1)

    @pl.when(has_lower)
    def _():
        for c in range(CHUNKS):
            send_e(c, el_ref).start()

    kinds = perm_ref.shape[0]
    offset = kinds - freq_ref.shape[0]
    ones = jnp.ones((8, deep), F32)
    tables = []
    for kind in range(kinds):
        if kind < offset:
            g, w2, drive = 0.0 * ones, 0.0 * ones, 0.0 * ones
        else:
            p = kind - offset
            g = damp_ref[p] * ones
            w2 = (freq_ref[p] * ones) * freq_ref[p]
            drive = strength_ref[p] * w2
        divisor = 1.0 + 0.5 * DT * g
        tables.append(
            (
                (1.0 - 0.5 * DT * g) / divisor,
                DT * drive / divisor,
                DT * w2 / divisor,
                DT / (perm_ref[kind] * ones),
            )
        )

    loads[2].wait()
    for x in range(layers):

        def fill(b, carry, x=x):
            rows = pl.ds(pl.multiple_of(b * 8, 8), 8)
            q = matb[x, rows, :]
            for i in range(4):
                value = tables[0][i]
                for kind in range(1, kinds):
                    value = jnp.where(q == kind, tables[kind][i], value)
                coef[i, x, rows, :] = value
            zero = jnp.zeros_like(ones)
            for c in range(3):
                jb[c, x, rows, :] = zero
                pb[c, x, rows, :] = zero
            return carry

        lax.fori_loop(0, width // 8, fill, 0, unroll=2)

    loads[0].wait()
    loads[1].wait()

    def update_h(x, y, size):
        here, next_y = pl.ds(y, size), pl.ds(y + 1, size)
        spot = pl.ds(y + PAD, size)
        ex, ey, ez = eb[0, x, here, :], eb[1, x, here, :], eb[2, x, here, :]
        ex_y, ez_y = eb[0, x, next_y, :], eb[2, x, next_y, :]
        hb[0, x, spot, :] -= DT * ((ez_y - ez) - (ahead(ey) - ey))
        if x < top:
            ey_x, ez_x = eb[1, x + 1, here, :], eb[2, x + 1, here, :]
            hb[1, x, spot, :] -= DT * ((ahead(ex) - ex) - (ez_x - ez))
            hb[2, x, spot, :] -= DT * ((ey_x - ey) - (ex_y - ex))
        else:
            hb[1, x, spot, :] -= DT * ((ahead(ex) - ex) + ez)
            hb[2, x, spot, :] += DT * (ey + (ex_y - ex))

    def finish_h(y, size):
        here, spot = pl.ds(y, size), pl.ds(y + PAD, size)
        hb[1, top, spot, :] += DT * ge[1, here, :]
        hb[2, top, spot, :] -= DT * ge[0, here, :]

    def update_e(x, y, size):
        here = pl.ds(y, size)
        spot, last_y = pl.ds(y + PAD, size), pl.ds(y + PAD - 1, size)
        hx, hy, hz = hb[0, x, spot, :], hb[1, x, spot, :], hb[2, x, spot, :]
        hx_y, hz_y = hb[0, x, last_y, :], hb[2, x, last_y, :]
        if x > 0:
            dz = hz - hb[2, x - 1, spot, :]
            dy = hy - hb[1, x - 1, spot, :]
        else:
            dz, dy = hz, hy
        curl = (
            (hz - hz_y) - (hy - behind(hy)),
            (hx - behind(hx)) - dz,
            dy - (hx - hx_y),
        )
        retain, pulling = coef[0, x, here, :], coef[1, x, here, :]
        spring, step_e = coef[2, x, here, :], coef[3, x, here, :]
        for c in range(3):
            field, polar = eb[c, x, here, :], pb[c, x, here, :]
            current = retain * jb[c, x, here, :] + pulling * field - spring * polar
            jb[c, x, here, :] = current
            pb[c, x, here, :] = polar + DT * current
            eb[c, x, here, :] = field + step_e * (curl[c] - current)

    def finish_e(y, size):
        here = pl.ds(y, size)
        step_e = coef[3, 0, here, :]
        eb[1, 0, here, :] += step_e * gh[1, here, :]
        eb[2, 0, here, :] -= step_e * gh[0, here, :]

    def edge(update, x):
        def body(b, carry):
            update(x, pl.multiple_of(b * ROWS, ROWS), ROWS)
            return carry

        lax.fori_loop(0, width // ROWS, body, 0)

    def inner(update, xs, c):
        for x in xs:
            for y in range(c * chunk, (c + 1) * chunk, min(ROWS, chunk)):
                update(x, y, min(ROWS, chunk))

    def record(n, buf, base, source, c):
        total = jnp.zeros((pick.shape[0], width), F32)
        for x in range(layers):
            value = buf[source, x, pl.ds(base, width), :]
            high = value.astype(BF16)
            low = (value - high.astype(F32)).astype(BF16)
            total = total + lax.dot_general(
                pick[:, pl.ds(x * 2 * deep, 2 * deep)],
                jnp.concatenate([high, low], axis=1),
                (((1,), (1,)), ((), ())),
                preferred_element_type=F32,
            )
        planes[n, c] = total
        sums = []
        for m in range(nm):
            product = total[8 * m : 8 * m + layers, :] * mode_ref[3 - c, m]
            sums.append(jnp.sum(product, axis=0, keepdims=True))
        value = jnp.sum(jnp.concatenate(sums, axis=0), axis=1, keepdims=True)
        value = value if c in (0, 3) else -value
        here = lax.broadcasted_iota(jnp.int32, (nm, deep), 1) == n * 4 + c
        part[pl.ds(0, nm), :] = jnp.where(here, value, part[pl.ds(0, nm), :])

    spots = (CHUNKS // 3, (2 * CHUNKS) // 3)

    def step(n, carry):
        @pl.when(has_upper & (n > 0))
        def _():
            for c in range(CHUNKS):
                send_h(c).wait_send()

        edge(update_h, top)
        for c in range(CHUNKS):

            @pl.when(has_upper)
            def _(c=c):
                send_e(c, eb).wait_recv()
                finish_h(c * chunk, chunk)
                send_h(c).start()

            inner(update_h, range(top), c)
            if c in spots:

                @pl.when(n > 0)
                def _(c=c):
                    record(n - 1, eb, 0, spots.index(c), spots.index(c))

        @pl.when(has_lower)
        def _():
            for c in range(CHUNKS):
                send_e(c, eb).wait_send()

        edge(update_e, 0)
        for c in range(CHUNKS):

            @pl.when(has_lower)
            def _(c=c):
                send_h(c).wait_recv()
                finish_e(c * chunk, chunk)

                @pl.when(n < STEPS - 1)
                def _():
                    send_e(c, eb).start()

            inner(update_e, range(1, layers), c)
            if c in spots:
                record(n, hb, PAD, spots.index(c), 2 + spots.index(c))
        return carry

    lax.fori_loop(0, STEPS, step, 0)

    for c in range(2):
        record(STEPS - 1, eb, 0, c, c)

    def share(k, slot):
        return pltpu.make_async_remote_copy(
            src_ref=part,
            dst_ref=gathered.at[slot],
            send_sem=sp_sem.at[k],
            recv_sem=rp_sem.at[k],
            device_id={"gx": lax.rem(me + k, count)},
            device_id_type=MESH,
        )

    for k in range(1, count):
        share(k, me).start()
    gathered[me] = part[...]

    to_scalars = pltpu.make_async_copy(rot, rot_s, rot_sem)
    to_scalars.start()

    @pl.when(has_upper)
    def _():
        for c in range(CHUNKS):
            send_h(c).wait_send()

    to_scalars.wait()
    for c in range(4):

        def fold(m, carry, c=c):
            rows = pl.ds(pl.multiple_of(8 * m, 8), layers)
            plane = [planes[n, c, rows, :] for n in range(STEPS)]
            for r in range(2):
                for f in range(nf):
                    value = rot_s[r, f, c] * plane[0]
                    for n in range(1, STEPS):
                        value = value + rot_s[r, f, n * 4 + c] * plane[n]
                    mon_ref[r, c, f, m] = value
            return carry

        lax.fori_loop(0, nm, fold, 0)

    for k in range(1, count):
        share(k, lax.rem(me - k + count, count)).wait()
    full = gathered[0]
    for k in range(1, count):
        full = full + gathered[k]
    for r in range(2):
        out = lax.dot_general(
            full,
            rot[r],
            (((1,), (1,)), ((), ())),
            preferred_element_type=F32,
            precision=lax.Precision.HIGHEST,
        )
        inter_ref[r] = scale * out[:nm, :]


def place_kernel(eb, hb, mon, inter, el_out, ma_out, mon_out, inter_out, sems):
    width = el_out.shape[2]
    copies = [
        pltpu.make_async_copy(eb.at[:, :, pl.ds(0, width)], el_out, sems.at[0]),
        pltpu.make_async_copy(hb.at[:, :, pl.ds(PAD, width)], ma_out, sems.at[1]),
        pltpu.make_async_copy(mon, mon_out, sems.at[2]),
        pltpu.make_async_copy(inter, inter_out, sems.at[3]),
    ]
    for copy in copies:
        copy.start()
    for copy in copies:
        copy.wait()


def on_device(
    electric,
    magnetic,
    material,
    permittivity,
    pole_frequency,
    pole_damping,
    pole_strength,
    frequencies,
    plane_depth,
    mode_fields,
):
    count = lax.axis_size("gx")
    layers, width, deep = material.shape
    nm, nf = plane_depth.shape[0], frequencies.shape[0]
    scale = 1.0 / math.sqrt(4.0 * layers * count * width)

    smem = pl.BlockSpec(memory_space=pltpu.SMEM)
    vmem = pl.BlockSpec(memory_space=pltpu.VMEM)
    hbm = pl.BlockSpec(memory_space=pl.ANY)
    field = (3, layers, width, deep)
    padded = (3, layers, width + PAD, deep)
    final = (field, field, (2, 4, nf, nm, layers, width), (2, nm, nf))
    kept = 4 * (2 * math.prod(padded) + math.prod(final[2])) + 2**16
    dma = pltpu.SemaphoreType.DMA
    held = pl.pallas_call(
        functools.partial(main_kernel, count, scale),
        out_shape=tuple(pltpu.VMEM(shape, F32) for shape in (padded, padded) + final[2:]),
        in_specs=[smem] * 6 + [vmem] + [hbm] * 3,
        out_specs=(vmem,) * 4,
        scratch_shapes=[
            pltpu.VMEM((2, width, deep), F32),
            pltpu.VMEM((2, width, deep), F32),
            pltpu.VMEM(field, F32),
            pltpu.VMEM(field, F32),
            pltpu.VMEM((4, layers, width, deep), F32),
            pltpu.VMEM((layers, width, deep), jnp.int32),
            pltpu.VMEM((STEPS, 4, 8 * nm, width), F32),
            pltpu.VMEM((8 * nm, layers * 2 * deep), BF16),
            pltpu.VMEM((8, deep), F32),
            pltpu.VMEM((count, 8, deep), F32),
            pltpu.VMEM((2, nf, deep), F32),
            pltpu.SMEM((2, nf, deep), F32),
            dma((3,)),
            dma,
            dma((CHUNKS,)),
            dma((CHUNKS,)),
            dma((CHUNKS,)),
            dma((CHUNKS,)),
            dma((count,)),
            dma((count,)),
        ],
        compiler_params=pltpu.CompilerParams(
            collective_id=0, has_side_effects=True, vmem_limit_bytes=VMEM_BYTES - kept
        ),
    )(
        permittivity,
        pole_frequency,
        pole_damping,
        pole_strength,
        frequencies,
        plane_depth,
        mode_fields,
        *(pltpu.with_memory_space_constraint(a, pltpu.HBM) for a in (electric, magnetic, material)),
    )
    return pl.pallas_call(
        place_kernel,
        out_shape=tuple(jax.ShapeDtypeStruct(shape, F32) for shape in final),
        in_specs=[vmem] * 4,
        out_specs=(hbm,) * 4,
        scratch_shapes=[dma((4,))],
        compiler_params=pltpu.CompilerParams(vmem_limit_bytes=16 * 2**20),
    )(*held)


def solution(mesh):
    in_specs = (
        P(None, "gx", None, None),
        P(None, "gx", None, None),
        P(("member", "gx"), None, None),
        P(),
        P(),
        P(),
        P(),
        P(),
        P(),
        P(None, None, "gx", None),
    )
    out_specs = (
        P(None, ("member", "gx"), None, None),
        P(None, ("member", "gx"), None, None),
        P(None, None, None, None, ("member", "gx"), None),
        P("member", None, None),
    )
    return jax.shard_map(
        on_device, mesh=mesh, in_specs=in_specs, out_specs=out_specs, check_vma=False
    )
```

profile of v0, /device:TPU:0, one launch (start us, length us, event | category | flops | bytes accessed | tf_op | source)
XLA Modules:
  0.0 51.8 jit_solution(13050018036487776110)
XLA Ops:
  0.6 49.1 %shard_map.129 = (f32[3,4,264,128]{3,2,1,0:T(8,128)S(1)}, f32[3,4,264,128]{3,2,1,0:T(8,128)S(1)}, f32[2,4,8,4,4,256]{5,4,3,2,1,0:T(4,128)S(1)}, f32[2,4,8]{2,1,0:T(4,128)S(1)}) custom-call(f32[4]{0:T(128)} %perm_ref.1, f32[2]{0:T(128)} %freq_ref.1, f32[2]{0:T(128)} %damp_ref.1, f32[2]{0:T(128)} %strength_ref.1, f32[8]{0:T(128)} %omega_ref.1, s32[4]{0:T(128)} %depth_ref.1, ...), custom_call_target="tpu_custom_call" | custom-call | tf_op jit(solution)/shard_map/pallas_call | solution.py:418
  49.7 2.0 %shard_map.130 = (f32[3,4,256,128]{3,2,1,0:T(8,128)}, f32[3,4,256,128]{3,2,1,0:T(8,128)}, f32[2,4,8,4,4,256]{5,4,3,2,1,0:T(4,128)}, f32[2,4,8]{2,1,0:T(4,128)}) custom-call(f32[3,4,264,128]{3,2,1,0:T(8,128)S(1)} %get-tuple-element.8.eb, f32[3,4,264,128]{3,2,1,0:T(8,128)S(1)} %get-tuple-element.9.hb, f32[2,4,8,4,4,256]{5,4,3,2,1,0:T(4,128)S(1)} %get-tuple-element.10.mon, ...), custom_call_target="tpu_custom_call" | custom-call | tf_op jit(solution)/shard_map/pallas_call | solution.py:458
where the time goes:
time: 51.9 us; the launch traced here: 51.8 us
  Pallas kernels  51.1 us (98%)
  between operations  0.64 us (1%)
    pallas_call x1, Pallas kernels, on_device(): pl.pallas_call(functools.partial(main_kernel, count, scale), out_shape=tu...  49.1 us
    pallas_call x1, Pallas kernels, on_device(): pl.pallas_call(place_kernel, out_shape=tuple((jax.ShapeDtypeStruct(shape,...  2.05 us

commit v1 on v0

--- a/solution.py
+++ b/solution.py
@@ -49,6 +49,7 @@
     inter_ref,
     ge,
     gh,
+    ph,
     jb,
     pb,
     coef,
@@ -67,6 +68,7 @@
     rh_sem,
     sp_sem,
     rp_sem,
+    met_sem,
 ):
     me = lax.axis_index("gx")
     layers, width, deep = mat_ref.shape
@@ -77,39 +79,86 @@
     top = layers - 1
 
     barrier = pltpu.get_barrier_semaphore()
-    for k in range(1, count):
-        pl.semaphore_signal(
-            barrier, inc=1, device_id={"gx": lax.rem(me + k, count)}, device_id_type=MESH
-        )
-
+    for present, side in ((has_lower, me - 1), (has_upper, me + 1)):
+
+        @pl.when(present)
+        def _(side=side):
+            pl.semaphore_signal(barrier, inc=1, device_id={"gx": side}, device_id_type=MESH)
+
+    rest = pl.ds(0, top)
     loads = [
-        pltpu.make_async_copy(el_ref, eb.at[:, :, pl.ds(0, width)], in_sem.at[0]),
-        pltpu.make_async_copy(ma_ref, hb.at[:, :, pl.ds(PAD, width)], in_sem.at[1]),
+        pltpu.make_async_copy(el_ref.at[:, top], eb.at[:, top, pl.ds(0, width)], in_sem.at[0]),
+        pltpu.make_async_copy(ma_ref.at[:, top], hb.at[:, top, pl.ds(PAD, width)], in_sem.at[1]),
         pltpu.make_async_copy(mat_ref, matb, in_sem.at[2]),
+        pltpu.make_async_copy(
+            el_ref.at[:, rest], eb.at[:, rest, pl.ds(0, width)], in_sem.at[3]
+        ),
+        pltpu.make_async_copy(
+            ma_ref.at[:, rest], hb.at[:, rest, pl.ds(PAD, width)], in_sem.at[4]
+        ),
     ]
     for load in loads:
         load.start()
 
-    def send_e(c, source):
+    def send_e(c, source, slot):
         rows = pl.ds(c * chunk, chunk)
         return pltpu.make_async_remote_copy(
             src_ref=source.at[pl.ds(1, 2), 0, rows],
-            dst_ref=ge.at[:, rows],
+            dst_ref=ge.at[slot, :, rows],
             send_sem=se_sem.at[c],
-            recv_sem=re_sem.at[c],
+            recv_sem=re_sem.at[slot, c],
             device_id={"gx": me - 1},
             device_id_type=MESH,
         )
 
-    def send_h(c):
+    def send_h(c, slot):
+        rows = pl.ds(c * chunk, chunk)
         return pltpu.make_async_remote_copy(
-            src_ref=hb.at[pl.ds(1, 2), top, pl.ds(PAD + c * chunk, chunk)],
-            dst_ref=gh.at[:, pl.ds(c * chunk, chunk)],
+            src_ref=ph.at[:, rows],
+            dst_ref=gh.at[slot, :, rows],
             send_sem=sh_sem.at[c],
-            recv_sem=rh_sem.at[c],
+            recv_sem=rh_sem.at[slot, c],
             device_id={"gx": me + 1},
             device_id_type=MESH,
         )
+
+    zero_rows = jnp.zeros((PAD, deep), F32)
+    for c in range(3):
+        for x in range(layers):
+            eb[c, x, pl.ds(width, PAD), :] = zero_rows
+            hb[c, x, pl.ds(0, PAD), :] = zero_rows
+    part[...] = jnp.zeros_like(part)
+
+    pl.semaphore_wait(barrier, has_lower.astype(jnp.int32) + has_upper.astype(jnp.int32))
+
+    @pl.when(has_lower)
+    def _():
+        for c in range(CHUNKS):
+            send_e(c, el_ref, 0).start()
+
+    @pl.when(~has_upper)
+    def _():
+        ge[...] = jnp.zeros_like(ge)
+
+    @pl.when(~has_lower)
+    def _():
+        gh[...] = jnp.zeros_like(gh)
+
+    def partial_h(y, size):
+        here, next_y, spot = pl.ds(y, size), pl.ds(y + 1, size), pl.ds(y + PAD, size)
+        ex, ey, ez = eb[0, top, here, :], eb[1, top, here, :], eb[2, top, here, :]
+        ex_y = eb[0, top, next_y, :]
+        ph[0, here, :] = hb[1, top, spot, :] - DT * ((ahead(ex) - ex) + ez)
+        ph[1, here, :] = hb[2, top, spot, :] + DT * (ey + (ex_y - ex))
+
+    loads[0].wait()
+    loads[1].wait()
+    for c in range(CHUNKS):
+        partial_h(c * chunk, chunk)
+
+        @pl.when(has_upper)
+        def _(c=c):
+            send_h(c, 0).start()
 
     shape = pick.shape
     row = lax.broadcasted_iota(jnp.int32, shape, 0)
@@ -129,20 +178,6 @@
     phase = ((lane // 4).astype(F32) + late) * DT * omega
     rot[0] = jnp.where(lane < 4 * STEPS, jnp.cos(phase), 0.0)
     rot[1] = jnp.where(lane < 4 * STEPS, -jnp.sin(phase), 0.0)
-
-    zero_rows = jnp.zeros((PAD, deep), F32)
-    for c in range(3):
-        for x in range(layers):
-            eb[c, x, pl.ds(width, PAD), :] = zero_rows
-            hb[c, x, pl.ds(0, PAD), :] = zero_rows
-    part[...] = jnp.zeros_like(part)
-
-    pl.semaphore_wait(barrier, count - 1)
-
-    @pl.when(has_lower)
-    def _():
-        for c in range(CHUNKS):
-            send_e(c, el_ref).start()
 
     kinds = perm_ref.shape[0]
     offset = kinds - freq_ref.shape[0]
@@ -185,8 +220,10 @@
 
         lax.fori_loop(0, width // 8, fill, 0, unroll=2)
 
-    loads[0].wait()
-    loads[1].wait()
+    loads[3].wait()
+    loads[4].wait()
+
+    lower = jnp.where(has_lower, DT, 0.0)
 
     def update_h(x, y, size):
         here, next_y = pl.ds(y, size), pl.ds(y + 1, size)
@@ -198,16 +235,13 @@
             ey_x, ez_x = eb[1, x + 1, here, :], eb[2, x + 1, here, :]
             hb[1, x, spot, :] -= DT * ((ahead(ex) - ex) - (ez_x - ez))
             hb[2, x, spot, :] -= DT * ((ey_x - ey) - (ex_y - ex))
-        else:
-            hb[1, x, spot, :] -= DT * ((ahead(ex) - ex) + ez)
-            hb[2, x, spot, :] += DT * (ey + (ex_y - ex))
-
-    def finish_h(y, size):
+
+    def finish_h(slot, y, size):
         here, spot = pl.ds(y, size), pl.ds(y + PAD, size)
-        hb[1, top, spot, :] += DT * ge[1, here, :]
-        hb[2, top, spot, :] -= DT * ge[0, here, :]
-
-    def update_e(x, y, size):
+        hb[1, top, spot, :] = ph[0, here, :] + DT * ge[slot, 1, here, :]
+        hb[2, top, spot, :] = ph[1, here, :] - DT * ge[slot, 0, here, :]
+
+    def update_e(x, y, size, slot):
         here = pl.ds(y, size)
         spot, last_y = pl.ds(y + PAD, size), pl.ds(y + PAD - 1, size)
         hx, hy, hz = hb[0, x, spot, :], hb[1, x, spot, :], hb[2, x, spot, :]
@@ -216,7 +250,8 @@
             dz = hz - hb[2, x - 1, spot, :]
             dy = hy - hb[1, x - 1, spot, :]
         else:
-            dz, dy = hz, hy
+            dz = hz - (gh[slot, 1, here, :] - lower * eb[1, 0, here, :])
+            dy = hy - (gh[slot, 0, here, :] + lower * eb[2, 0, here, :])
         curl = (
             (hz - hz_y) - (hy - behind(hy)),
             (hx - behind(hx)) - dz,
@@ -231,28 +266,18 @@
             pb[c, x, here, :] = polar + DT * current
             eb[c, x, here, :] = field + step_e * (curl[c] - current)
 
-    def finish_e(y, size):
-        here = pl.ds(y, size)
-        step_e = coef[3, 0, here, :]
-        eb[1, 0, here, :] += step_e * gh[1, here, :]
-        eb[2, 0, here, :] -= step_e * gh[0, here, :]
-
-    def edge(update, x):
-        def body(b, carry):
-            update(x, pl.multiple_of(b * ROWS, ROWS), ROWS)
-            return carry
-
-        lax.fori_loop(0, width // ROWS, body, 0)
-
-    def inner(update, xs, c):
+    def sweep(update, xs, c, *args):
+        size = min(ROWS, chunk)
         for x in xs:
-            for y in range(c * chunk, (c + 1) * chunk, min(ROWS, chunk)):
-                update(x, y, min(ROWS, chunk))
-
-    def record(n, buf, base, source, c):
-        total = jnp.zeros((pick.shape[0], width), F32)
+            for y in range(c * chunk, (c + 1) * chunk, size):
+                update(x, y, size, *args)
+
+    def record(n, part_of, buf, base, source, c):
+        size = width // 2
+        cols = pl.ds(part_of * size, size)
+        total = jnp.zeros((pick.shape[0], size), F32)
         for x in range(layers):
-            value = buf[source, x, pl.ds(base, width), :]
+            value = buf[source, x, pl.ds(base + part_of * size, size), :]
             high = value.astype(BF16)
             low = (value - high.astype(F32)).astype(BF16)
             total = total + lax.dot_general(
@@ -261,66 +286,96 @@
                 (((1,), (1,)), ((), ())),
                 preferred_element_type=F32,
             )
-        planes[n, c] = total
+        planes[n, c, :, cols] = total
         sums = []
         for m in range(nm):
-            product = total[8 * m : 8 * m + layers, :] * mode_ref[3 - c, m]
+            product = total[8 * m : 8 * m + layers, :] * mode_ref[3 - c, m, :, cols]
             sums.append(jnp.sum(product, axis=0, keepdims=True))
         value = jnp.sum(jnp.concatenate(sums, axis=0), axis=1, keepdims=True)
         value = value if c in (0, 3) else -value
         here = lax.broadcasted_iota(jnp.int32, (nm, deep), 1) == n * 4 + c
-        part[pl.ds(0, nm), :] = jnp.where(here, value, part[pl.ds(0, nm), :])
-
-    spots = (CHUNKS // 3, (2 * CHUNKS) // 3)
+        kept = part[pl.ds(0, nm), :]
+        part[pl.ds(0, nm), :] = kept + jnp.where(here, value, 0.0)
+
+    def record_all(n, part_of):
+        for c in range(2):
+            record(n, part_of, eb, 0, c, c)
+            record(n, part_of, hb, PAD, c, 2 + c)
+
+    reach = [d for d in (4 << i for i in range(count.bit_length())) if d < count]
+
+    def greet(i):
+        for present, side in ((me >= reach[i], me - reach[i]), (me < count - reach[i], me + reach[i])):
+
+            @pl.when(present)
+            def _(side=side):
+                pl.semaphore_signal(
+                    met_sem.at[i], inc=1, device_id={"gx": side}, device_id_type=MESH
+                )
+
+    def met(i):
+        peers = sum(p.astype(jnp.int32) for p in (me >= reach[i], me < count - reach[i]))
+        pl.semaphore_wait(met_sem.at[i], peers)
+
+    def send_up(n, c, slot):
+        @pl.when(has_upper)
+        def _():
+            send_h(c, slot).wait_send()
+
+        @pl.when(n < STEPS - 1)
+        def _():
+            partial_h(c * chunk, chunk)
+
+            @pl.when(has_upper)
+            def _():
+                send_h(c, slot).start()
 
     def step(n, carry):
-        @pl.when(has_upper & (n > 0))
-        def _():
-            for c in range(CHUNKS):
-                send_h(c).wait_send()
-
-        edge(update_h, top)
+        slot = lax.rem(n, 2)
+        other = 1 - slot
         for c in range(CHUNKS):
+            sweep(update_h, range(layers), c)
 
             @pl.when(has_upper)
             def _(c=c):
-                send_e(c, eb).wait_recv()
-                finish_h(c * chunk, chunk)
-                send_h(c).start()
-
-            inner(update_h, range(top), c)
-            if c in spots:
-
-                @pl.when(n > 0)
-                def _(c=c):
-                    record(n - 1, eb, 0, spots.index(c), spots.index(c))
-
-        @pl.when(has_lower)
-        def _():
-            for c in range(CHUNKS):
-                send_e(c, eb).wait_send()
-
-        edge(update_e, 0)
-        for c in range(CHUNKS):
+                send_e(c, eb, slot).wait_recv()
 
             @pl.when(has_lower)
             def _(c=c):
-                send_h(c).wait_recv()
-                finish_e(c * chunk, chunk)
-
-                @pl.when(n < STEPS - 1)
-                def _():
-                    send_e(c, eb).start()
-
-            inner(update_e, range(1, layers), c)
-            if c in spots:
-                record(n, hb, PAD, spots.index(c), 2 + spots.index(c))
+                send_h(c, slot).wait_recv()
+                send_e(c, eb, slot).wait_send()
+
+            finish_h(slot, c * chunk, chunk)
+            sweep(update_e, (0, top), c, slot)
+
+            @pl.when(has_lower & (n < STEPS - 1))
+            def _(c=c):
+                send_e(c, eb, other).start()
+
+            if c > 0:
+                send_up(n, c - 1, other)
+            sweep(update_e, range(1, top), c, slot)
+            if c == CHUNKS // 2 - 1:
+                record_all(n, 0)
+        send_up(n, CHUNKS - 1, other)
+        record_all(n, 1)
+        for i in range(min(len(reach), STEPS - 3)):
+
+            @pl.when(n == i + 2)
+            def _(i=i):
+                if i > 0:
+                    met(i - 1)
+                greet(i)
+
         return carry
 
     lax.fori_loop(0, STEPS, step, 0)
 
-    for c in range(2):
-        record(STEPS - 1, eb, 0, c, c)
+    begun = min(len(reach), STEPS - 3)
+    for i in range(max(begun - 1, 0), len(reach)):
+        if i >= begun:
+            greet(i)
+        met(i)
 
     def share(k, slot):
         return pltpu.make_async_remote_copy(
@@ -338,11 +393,6 @@
 
     to_scalars = pltpu.make_async_copy(rot, rot_s, rot_sem)
     to_scalars.start()
-
-    @pl.when(has_upper)
-    def _():
-        for c in range(CHUNKS):
-            send_h(c).wait_send()
 
     to_scalars.wait()
     for c in range(4):
@@ -421,7 +471,8 @@
         in_specs=[smem] * 6 + [vmem] + [hbm] * 3,
         out_specs=(vmem,) * 4,
         scratch_shapes=[
-            pltpu.VMEM((2, width, deep), F32),
+            pltpu.VMEM((2, 2, width, deep), F32),
+            pltpu.VMEM((2, 2, width, deep), F32),
             pltpu.VMEM((2, width, deep), F32),
             pltpu.VMEM(field, F32),
             pltpu.VMEM(field, F32),
@@ -433,14 +484,15 @@
             pltpu.VMEM((count, 8, deep), F32),
             pltpu.VMEM((2, nf, deep), F32),
             pltpu.SMEM((2, nf, deep), F32),
-            dma((3,)),
+            dma((5,)),
             dma,
             dma((CHUNKS,)),
+            dma((2, CHUNKS)),
             dma((CHUNKS,)),
-            dma((CHUNKS,)),
-            dma((CHUNKS,)),
+            dma((2, CHUNKS)),
             dma((count,)),
             dma((count,)),
+            pltpu.SemaphoreType.REGULAR((count.bit_length(),)),
         ],
         compiler_params=pltpu.CompilerParams(
             collective_id=0, has_side_effects=True, vmem_limit_bytes=VMEM_BYTES - kept

time: 51.9 us -> 49.1 us (0.946)
  Pallas kernels: 51.1 us -> 48.3 us
    pallas_call x1, Pallas kernels: 49.1 us -> 46.2 us  [on_device(): pl.pallas_call(functools.partial(main_kernel, count, scale), out_shape=tu...]
where the time goes in v1:
time: 49.1 us; the launch traced here: 48.9 us
  Pallas kernels  48.3 us (98%)
  between operations  0.64 us (1%)
    pallas_call x1, Pallas kernels, on_device(): pl.pallas_call(functools.partial(main_kernel, count, scale), out_shape=tu...  46.2 us
    pallas_call x1, Pallas kernels, on_device(): pl.pallas_call(place_kernel, out_shape=tuple((jax.ShapeDtypeStruct(shape,...  2.05 us

profile of v1, /device:TPU:0, one launch (start us, length us, event | category | flops | bytes accessed | tf_op | source)
XLA Modules:
  0.0 48.9 jit_solution(11125143365504721256)
XLA Ops:
  0.6 46.2 %shard_map.129 = (f32[3,4,264,128]{3,2,1,0:T(8,128)S(1)}, f32[3,4,264,128]{3,2,1,0:T(8,128)S(1)}, f32[2,4,8,4,4,256]{5,4,3,2,1,0:T(4,128)S(1)}, f32[2,4,8]{2,1,0:T(4,128)S(1)}) custom-call(f32[4]{0:T(128)} %perm_ref.1, f32[2]{0:T(128)} %freq_ref.1, f32[2]{0:T(128)} %damp_ref.1, f32[2]{0:T(128)} %strength_ref.1, f32[8]{0:T(128)} %omega_ref.1, s32[4]{0:T(128)} %depth_ref.1, ...), custom_call_target="tpu_custom_call" | custom-call | tf_op jit(solution)/shard_map/pallas_call | solution.py:468
  46.9 2.0 %shard_map.130 = (f32[3,4,256,128]{3,2,1,0:T(8,128)}, f32[3,4,256,128]{3,2,1,0:T(8,128)}, f32[2,4,8,4,4,256]{5,4,3,2,1,0:T(4,128)}, f32[2,4,8]{2,1,0:T(4,128)}) custom-call(f32[3,4,264,128]{3,2,1,0:T(8,128)S(1)} %get-tuple-element.8.eb, f32[3,4,264,128]{3,2,1,0:T(8,128)S(1)} %get-tuple-element.9.hb, f32[2,4,8,4,4,256]{5,4,3,2,1,0:T(4,128)S(1)} %get-tuple-element.10.mon, ...), custom_call_target="tpu_custom_call" | custom-call | tf_op jit(solution)/shard_map/pallas_call | solution.py:510

commit v2 on v1

--- a/solution.py
+++ b/solution.py
@@ -45,7 +45,8 @@
     mat_ref,
     eb,
     hb,
-    mon_ref,
+    planes,
+    rot,
     inter_ref,
     ge,
     gh,
@@ -54,20 +55,25 @@
     pb,
     coef,
     matb,
-    planes,
     pick,
+    modes,
+    fixed,
+    memory,
+    near,
+    give_up,
+    give_down,
+    from_down,
+    from_up,
     part,
     gathered,
-    rot,
-    rot_s,
     in_sem,
-    rot_sem,
     se_sem,
     re_sem,
     sh_sem,
     rh_sem,
     sp_sem,
     rp_sem,
+    wt_sem,
     met_sem,
 ):
     me = lax.axis_index("gx")
@@ -139,10 +145,12 @@
     @pl.when(~has_upper)
     def _():
         ge[...] = jnp.zeros_like(ge)
+        from_up[...] = jnp.zeros_like(from_up)
 
     @pl.when(~has_lower)
     def _():
         gh[...] = jnp.zeros_like(gh)
+        from_down[...] = jnp.zeros_like(from_down)
 
     def partial_h(y, size):
         here, next_y, spot = pl.ds(y, size), pl.ds(y + 1, size), pl.ds(y + PAD, size)
@@ -160,14 +168,25 @@
         def _(c=c):
             send_h(c, 0).start()
 
+    rows = 8 * nm
     shape = pick.shape
     row = lax.broadcasted_iota(jnp.int32, shape, 0)
     col = lax.broadcasted_iota(jnp.int32, shape, 1)
+    spot_of = lax.rem(row, rows)
     wanted = jnp.zeros(shape, jnp.int32)
     for m in range(nm):
-        wanted = jnp.where(row // 8 == m, depth_ref[m], wanted)
+        wanted = jnp.where(spot_of // 8 == m, depth_ref[m], wanted)
+    wanted = jnp.where(row // rows == 1, wanted - 1, wanted)
+    wanted = jnp.where(row // rows == 2, wanted + 1, wanted)
     hit = (row % 8 == col // (2 * deep)) & (col % deep == wanted)
     pick[...] = jnp.where(hit, 1.0, 0.0).astype(BF16)
+
+    for c in range(4):
+        for m in range(nm):
+            value = mode_ref[3 - c, m]
+            value = value if c in (0, 3) else -value
+            value = jnp.concatenate([value, jnp.zeros((8 - layers, width), F32)], axis=0)
+            modes[c, pl.ds(8 * m, 8), :] = value
 
     lane = lax.broadcasted_iota(jnp.int32, (nf, deep), 1)
     line = lax.broadcasted_iota(jnp.int32, (nf, deep), 0)
@@ -225,6 +244,71 @@
 
     lower = jnp.where(has_lower, DT, 0.0)
 
+    def select(value_of, groups, size):
+        total = jnp.zeros((groups * rows, size), F32)
+        for x in range(layers):
+            value = value_of(x)
+            high = value.astype(BF16)
+            low = (value - high.astype(F32)).astype(BF16)
+            total = total + lax.dot_general(
+                pick[pl.ds(0, groups * rows), pl.ds(x * 2 * deep, 2 * deep)],
+                jnp.concatenate([high, low], axis=1),
+                (((1,), (1,)), ((), ())),
+                preferred_element_type=F32,
+            )
+        return total
+
+    for i in range(4):
+        fixed[i] = select(lambda x, i=i: coef[i, x], 1, width)
+    for c in range(2):
+        near[c, pl.ds(0, rows), :] = select(
+            lambda x, c=c: eb[c, x, pl.ds(0, width), :], 1, width
+        )
+    memory[...] = jnp.zeros_like(memory)
+
+    line = lax.broadcasted_iota(jnp.int32, (rows, width), 0) % 8
+
+    def placed(values):
+        total = jnp.zeros((rows, width), F32)
+        for at, (value, source) in enumerate(values):
+            if at != source:
+                value = pltpu.roll(value, (at - source) % rows, 0)
+            total = jnp.where(line == at, value, total)
+        return total
+
+    give_up[...] = placed(
+        [(modes[3], top), (fixed[3] * modes[0], top), (fixed[3] * modes[1], top)]
+    ).reshape(give_up.shape)
+    give_down[...] = placed([(fixed[3] * modes[1], 0)]).reshape(give_down.shape)
+
+    def weights_up():
+        return pltpu.make_async_remote_copy(
+            src_ref=give_up.at[:, pl.ds(0, 4)],
+            dst_ref=from_down.at[:, pl.ds(0, 4)],
+            send_sem=wt_sem.at[0],
+            recv_sem=wt_sem.at[1],
+            device_id={"gx": me + 1},
+            device_id_type=MESH,
+        )
+
+    def weights_down():
+        return pltpu.make_async_remote_copy(
+            src_ref=give_down.at[:, pl.ds(0, 4)],
+            dst_ref=from_up.at[:, pl.ds(0, 4)],
+            send_sem=wt_sem.at[2],
+            recv_sem=wt_sem.at[3],
+            device_id={"gx": me - 1},
+            device_id_type=MESH,
+        )
+
+    @pl.when(has_upper)
+    def _():
+        weights_up().start()
+
+    @pl.when(has_lower)
+    def _():
+        weights_down().start()
+
     def update_h(x, y, size):
         here, next_y = pl.ds(y, size), pl.ds(y + 1, size)
         spot = pl.ds(y + PAD, size)
@@ -272,35 +356,94 @@
             for y in range(c * chunk, (c + 1) * chunk, size):
                 update(x, y, size, *args)
 
+    def note(n, c, product):
+        sums = jnp.sum(product.reshape(nm, 8, product.shape[1]), axis=1)
+        value = jnp.sum(sums, axis=1, keepdims=True)
+        here = lax.broadcasted_iota(jnp.int32, (nm, deep), 1) == n * 4 + c
+        kept = part[pl.ds(0, nm), :]
+        part[pl.ds(0, nm), :] = kept + jnp.where(here, value, 0.0)
+
     def record(n, part_of, buf, base, source, c):
         size = width // 2
         cols = pl.ds(part_of * size, size)
-        total = jnp.zeros((pick.shape[0], size), F32)
-        for x in range(layers):
-            value = buf[source, x, pl.ds(base + part_of * size, size), :]
-            high = value.astype(BF16)
-            low = (value - high.astype(F32)).astype(BF16)
-            total = total + lax.dot_general(
-                pick[:, pl.ds(x * 2 * deep, 2 * deep)],
-                jnp.concatenate([high, low], axis=1),
-                (((1,), (1,)), ((), ())),
-                preferred_element_type=F32,
-            )
-        planes[n, c, :, cols] = total
-        sums = []
-        for m in range(nm):
-            product = total[8 * m : 8 * m + layers, :] * mode_ref[3 - c, m, :, cols]
-            sums.append(jnp.sum(product, axis=0, keepdims=True))
-        value = jnp.sum(jnp.concatenate(sums, axis=0), axis=1, keepdims=True)
-        value = value if c in (0, 3) else -value
-        here = lax.broadcasted_iota(jnp.int32, (nm, deep), 1) == n * 4 + c
-        kept = part[pl.ds(0, nm), :]
-        part[pl.ds(0, nm), :] = kept + jnp.where(here, value, 0.0)
+        here = pl.ds(base + part_of * size, size)
+        last = isinstance(n, int)
+        total = select(lambda x: buf[source, x, here, :], 1 if last else 3, size)
+        planes[n, c, :, cols] = total[:rows, :]
+        if last:
+            return
+        note(n, c, total[:rows, :] * modes[c, :, cols])
+        if c < 2:
+            field = near[c, pl.ds(0, rows), cols]
+            polar = memory[1, c, :, cols]
+            current = fixed[0, :, cols] * memory[0, c, :, cols]
+            current = current + fixed[1, :, cols] * field - fixed[2, :, cols] * polar
+            memory[0, c, :, cols] = current
+            memory[1, c, :, cols] = polar + DT * current
+        near[c, :, cols] = total
 
     def record_all(n, part_of):
         for c in range(2):
             record(n, part_of, eb, 0, c, c)
             record(n, part_of, hb, PAD, c, 2 + c)
+        if isinstance(n, int):
+            return
+
+        @pl.when(n == STEPS - 2)
+        def _():
+            size = width // 2
+            cols = pl.ds(part_of * size, size)
+            for i, buf, base in ((4, eb, 0), (5, hb, PAD)):
+                here = pl.ds(base + part_of * size, size)
+                near[i, :, cols] = select(lambda x: buf[2, x, here, :], 3, size)
+
+    def foresee():
+        final = STEPS - 1
+
+        def at(i, group):
+            return near[i, pl.ds(group * rows, rows), :]
+
+        def above(value):
+            return jnp.where(line >= top, 0.0, pltpu.roll(value, rows - 1, 0))
+
+        ex, ex_last, ex_next = at(0, 0), at(0, 1), at(0, 2)
+        ey, ey_last, ey_next = at(1, 0), at(1, 1), at(1, 2)
+        ez, ez_last = at(4, 0), at(4, 1)
+        hx = at(2, 0) - DT * ((ahead(ez) - ez) - (ey_next - ey))
+        hx_last = at(2, 1) - DT * ((ahead(ez_last) - ez_last) - (ey - ey_last))
+        hy = at(3, 0) - DT * ((ex_next - ex) - (above(ez) - ez))
+        hy_last = at(3, 1) - DT * ((ex - ex_last) - (above(ez_last) - ez_last))
+        hz = at(5, 0) - DT * ((above(ey) - ey) - (ahead(ex) - ex))
+        hz_below = jnp.where(line == 0, -lower * ey, pltpu.roll(hz, 1, 0))
+        curl = (
+            (hz - behind(hz)) - (hy - hy_last),
+            (hx - hx_last) - (hz - hz_below),
+        )
+        for c, field in enumerate((ex, ey)):
+            current = fixed[0] * memory[0, c] + fixed[1] * field - fixed[2] * memory[1, c]
+            note(final, c, (field + fixed[3] * (curl[c] - current)) * modes[c])
+        note(final, 2, hx * modes[2])
+        note(final, 3, hy * modes[3])
+
+        @pl.when(has_upper)
+        def _():
+            weights_up().wait_send()
+            weights_down().wait_recv()
+
+        @pl.when(has_lower)
+        def _():
+            weights_down().wait_send()
+            weights_up().wait_recv()
+
+        def known(ref):
+            return jnp.where(line < 4, ref[...].reshape(rows, width), 0.0)
+
+        rise = jnp.where(line == 0, pltpu.roll(hz, rows - top, 0), 0.0)
+        note(final, 1, known(from_up) * rise)
+        step_x = (ey - behind(ey)) + (ez - ez_last)
+        fall = placed([(DT * ez, 0), (-DT * step_x, 0), (DT * ey, 0)]) * known(from_down)
+        for at_line, c in enumerate((3, 0, 1)):
+            note(final, c, jnp.where(line == at_line, fall, 0.0))
 
     reach = [d for d in (4 << i for i in range(count.bit_length())) if d < count]
 
@@ -322,16 +465,17 @@
         def _():
             send_h(c, slot).wait_send()
 
-        @pl.when(n < STEPS - 1)
+        if isinstance(n, int):
+            return
+        partial_h(c * chunk, chunk)
+
+        @pl.when(has_upper)
         def _():
-            partial_h(c * chunk, chunk)
-
-            @pl.when(has_upper)
-            def _():
-                send_h(c, slot).start()
+            send_h(c, slot).start()
 
     def step(n, carry):
-        slot = lax.rem(n, 2)
+        last = isinstance(n, int)
+        slot = n % 2 if last else lax.rem(n, 2)
         other = 1 - slot
         for c in range(CHUNKS):
             sweep(update_h, range(layers), c)
@@ -348,9 +492,11 @@
             finish_h(slot, c * chunk, chunk)
             sweep(update_e, (0, top), c, slot)
 
-            @pl.when(has_lower & (n < STEPS - 1))
-            def _(c=c):
-                send_e(c, eb, other).start()
+            if not last:
+
+                @pl.when(has_lower)
+                def _(c=c):
+                    send_e(c, eb, other).start()
 
             if c > 0:
                 send_up(n, c - 1, other)
@@ -359,6 +505,8 @@
                 record_all(n, 0)
         send_up(n, CHUNKS - 1, other)
         record_all(n, 1)
+        if last:
+            return carry
         for i in range(min(len(reach), STEPS - 3)):
 
             @pl.when(n == i + 2)
@@ -369,7 +517,8 @@
 
         return carry
 
-    lax.fori_loop(0, STEPS, step, 0)
+    lax.fori_loop(0, STEPS - 1, step, 0)
+    foresee()
 
     begun = min(len(reach), STEPS - 3)
     for i in range(max(begun - 1, 0), len(reach)):
@@ -391,24 +540,7 @@
         share(k, me).start()
     gathered[me] = part[...]
 
-    to_scalars = pltpu.make_async_copy(rot, rot_s, rot_sem)
-    to_scalars.start()
-
-    to_scalars.wait()
-    for c in range(4):
-
-        def fold(m, carry, c=c):
-            rows = pl.ds(pl.multiple_of(8 * m, 8), layers)
-            plane = [planes[n, c, rows, :] for n in range(STEPS)]
-            for r in range(2):
-                for f in range(nf):
-                    value = rot_s[r, f, c] * plane[0]
-                    for n in range(1, STEPS):
-                        value = value + rot_s[r, f, n * 4 + c] * plane[n]
-                    mon_ref[r, c, f, m] = value
-            return carry
-
-        lax.fori_loop(0, nm, fold, 0)
+    step(STEPS - 1, 0)
 
     for k in range(1, count):
         share(k, lax.rem(me - k + count, count)).wait()
@@ -426,16 +558,37 @@
         inter_ref[r] = scale * out[:nm, :]
 
 
-def place_kernel(eb, hb, mon, inter, el_out, ma_out, mon_out, inter_out, sems):
-    width = el_out.shape[2]
+def place_kernel(
+    eb, hb, planes, rot, inter, el_out, ma_out, mon_out, inter_out, mon, rot_s, sems, mon_sem
+):
+    layers, width = el_out.shape[1:3]
+    nf, nm = mon.shape[2:4]
+    to_scalars = pltpu.make_async_copy(rot, rot_s, sems.at[3])
+    to_scalars.start()
     copies = [
         pltpu.make_async_copy(eb.at[:, :, pl.ds(0, width)], el_out, sems.at[0]),
         pltpu.make_async_copy(hb.at[:, :, pl.ds(PAD, width)], ma_out, sems.at[1]),
-        pltpu.make_async_copy(mon, mon_out, sems.at[2]),
-        pltpu.make_async_copy(inter, inter_out, sems.at[3]),
+        pltpu.make_async_copy(inter, inter_out, sems.at[2]),
     ]
     for copy in copies:
         copy.start()
+    to_scalars.wait()
+    for c in range(4):
+
+        def fold(m, carry, c=c):
+            rows = pl.ds(pl.multiple_of(8 * m, 8), layers)
+            plane = [planes[n, c, rows, :] for n in range(STEPS)]
+            for r in range(2):
+                for f in range(nf):
+                    value = rot_s[r, f, c] * plane[0]
+                    for n in range(1, STEPS):
+                        value = value + rot_s[r, f, n * 4 + c] * plane[n]
+                    mon[r, c, f, m] = value
+            return carry
+
+        lax.fori_loop(0, nm, fold, 0)
+        copies.append(pltpu.make_async_copy(mon.at[:, c], mon_out.at[:, c], mon_sem.at[c]))
+        copies[-1].start()
     for copy in copies:
         copy.wait()
 
@@ -463,13 +616,15 @@
     field = (3, layers, width, deep)
     padded = (3, layers, width + PAD, deep)
     final = (field, field, (2, 4, nf, nm, layers, width), (2, nm, nf))
-    kept = 4 * (2 * math.prod(padded) + math.prod(final[2])) + 2**16
+    planar = (8 * nm, width)
+    shapes = (padded, padded, (STEPS, 4) + planar, (2, nf, deep), (2, nm, nf))
+    kept = 4 * sum(math.prod(shape) for shape in shapes[:3]) + 2**17
     dma = pltpu.SemaphoreType.DMA
     held = pl.pallas_call(
         functools.partial(main_kernel, count, scale),
-        out_shape=tuple(pltpu.VMEM(shape, F32) for shape in (padded, padded) + final[2:]),
+        out_shape=tuple(pltpu.VMEM(shape, F32) for shape in shapes),
         in_specs=[smem] * 6 + [vmem] + [hbm] * 3,
-        out_specs=(vmem,) * 4,
+        out_specs=(vmem,) * 5,
         scratch_shapes=[
             pltpu.VMEM((2, 2, width, deep), F32),
             pltpu.VMEM((2, 2, width, deep), F32),
@@ -478,20 +633,25 @@
             pltpu.VMEM(field, F32),
             pltpu.VMEM((4, layers, width, deep), F32),
             pltpu.VMEM((layers, width, deep), jnp.int32),
-            pltpu.VMEM((STEPS, 4, 8 * nm, width), F32),
-            pltpu.VMEM((8 * nm, layers * 2 * deep), BF16),
+            pltpu.VMEM((3 * 8 * nm, layers * 2 * deep), BF16),
+            pltpu.VMEM((4,) + planar, F32),
+            pltpu.VMEM((4,) + planar, F32),
+            pltpu.VMEM((2, 2) + planar, F32),
+            pltpu.VMEM((6, 3 * 8 * nm, width), F32),
+            pltpu.VMEM((nm, 8, width), F32),
+            pltpu.VMEM((nm, 8, width), F32),
+            pltpu.VMEM((nm, 8, width), F32),
+            pltpu.VMEM((nm, 8, width), F32),
             pltpu.VMEM((8, deep), F32),
             pltpu.VMEM((count, 8, deep), F32),
-            pltpu.VMEM((2, nf, deep), F32),
-            pltpu.SMEM((2, nf, deep), F32),
             dma((5,)),
-            dma,
             dma((CHUNKS,)),
             dma((2, CHUNKS)),
             dma((CHUNKS,)),
             dma((2, CHUNKS)),
             dma((count,)),
             dma((count,)),
+            dma((4,)),
             pltpu.SemaphoreType.REGULAR((count.bit_length(),)),
         ],
         compiler_params=pltpu.CompilerParams(
@@ -510,9 +670,14 @@
     return pl.pallas_call(
         place_kernel,
         out_shape=tuple(jax.ShapeDtypeStruct(shape, F32) for shape in final),
-        in_specs=[vmem] * 4,
+        in_specs=[vmem] * 5,
         out_specs=(hbm,) * 4,
-        scratch_shapes=[dma((4,))],
+        scratch_shapes=[
+            pltpu.VMEM(final[2], F32),
+            pltpu.SMEM((2, nf, deep), F32),
+            dma((4,)),
+            dma((4,)),
+        ],
         compiler_params=pltpu.CompilerParams(vmem_limit_bytes=16 * 2**20),
     )(*held)
 

time: 49.1 us -> 48.2 us (0.982)
  Pallas kernels: 48.3 us -> 47.4 us
    pallas_call x1, Pallas kernels: 46.2 us -> 44.9 us  [on_device(): pl.pallas_call(functools.partial(main_kernel, count, scale), out_shape=tu...]
    pallas_call x1, Pallas kernels: 2.05 us -> 2.55 us  [on_device(): pl.pallas_call(place_kernel, out_shape=tuple((jax.ShapeDtypeStruct(shape,...]
where the time goes in v2:
time: 48.2 us; the launch traced here: 48.1 us
  Pallas kernels  47.4 us (98%)
  between operations  0.64 us (1%)
    pallas_call x1, Pallas kernels, on_device(): pl.pallas_call(functools.partial(main_kernel, count, scale), out_shape=tu...  44.9 us
    pallas_call x1, Pallas kernels, on_device(): pl.pallas_call(place_kernel, out_shape=tuple((jax.ShapeDtypeStruct(shape,...  2.55 us

profile of v2, /device:TPU:0, one launch (start us, length us, event | category | flops | bytes accessed | tf_op | source)
XLA Modules:
  0.0 48.1 jit_solution(14731194065040081599)
XLA Ops:
  0.6 44.9 %shard_map.129 = (f32[3,4,264,128]{3,2,1,0:T(8,128)S(1)}, f32[3,4,264,128]{3,2,1,0:T(8,128)S(1)}, f32[6,4,32,256]{3,2,1,0:T(8,128)S(1)}, f32[2,8,128]{2,1,0:T(8,128)S(1)}, f32[2,4,8]{2,1,0:T(4,128)S(1)}) custom-call(f32[4]{0:T(128)} %perm_ref.1, f32[2]{0:T(128)} %freq_ref.1, f32[2]{0:T(128)} %damp_ref.1, f32[2]{0:T(128)} %strength_ref.1, f32[8]{0:T(128)} %omega_ref.1, ...), custom_call_target="tpu_custom_call" | custom-call | tf_op jit(solution)/shard_map/pallas_call | solution.py:623
  45.5 2.5 %shard_map.130 = (f32[3,4,256,128]{3,2,1,0:T(8,128)}, f32[3,4,256,128]{3,2,1,0:T(8,128)}, f32[2,4,8,4,4,256]{5,4,3,2,1,0:T(4,128)}, f32[2,4,8]{2,1,0:T(4,128)}) custom-call(f32[3,4,264,128]{3,2,1,0:T(8,128)S(1)} %get-tuple-element.9.eb, f32[3,4,264,128]{3,2,1,0:T(8,128)S(1)} %get-tuple-element.10.hb, f32[6,4,32,256]{3,2,1,0:T(8,128)S(1)} %get-tuple-element.11.planes, ...), custom_call_target="tpu_custom_call" | custom-call | tf_op jit(solution)/shard_map/pallas_call | solution.py:670

commit v3 on v2

--- a/solution.py
+++ b/solution.py
@@ -13,6 +13,7 @@
 CHUNKS = 8
 ROWS = 32
 PAD = 8
+HELD = 3
 MESH = pl.DeviceIdType.MESH
 VMEM_BYTES = 67043328
 F32 = jnp.float32
@@ -30,9 +31,24 @@
     return jnp.where(lane == 0, 0.0, pltpu.roll(value, 1, 1))
 
 
+def select(pick, layers, value_of, groups):
+    rows, span = pick.shape[0] // 3 * groups, pick.shape[1] // layers
+    total = 0.0
+    for x in range(layers):
+        value = value_of(x)
+        high = value.astype(BF16)
+        low = (value - high.astype(F32)).astype(BF16)
+        total = total + lax.dot_general(
+            pick[pl.ds(0, rows), pl.ds(x * span, span)],
+            jnp.concatenate([high, low], axis=1),
+            (((1,), (1,)), ((), ())),
+            preferred_element_type=F32,
+        )
+    return total
+
+
 def main_kernel(
     count,
-    scale,
     perm_ref,
     freq_ref,
     damp_ref,
@@ -45,9 +61,9 @@
     mat_ref,
     eb,
     hb,
-    planes,
+    mon,
     rot,
-    inter_ref,
+    full,
     ge,
     gh,
     ph,
@@ -56,6 +72,7 @@
     coef,
     matb,
     pick,
+    planes,
     modes,
     fixed,
     memory,
@@ -66,6 +83,8 @@
     from_up,
     part,
     gathered,
+    rot_s,
+    rot_sem,
     in_sem,
     se_sem,
     re_sem,
@@ -244,25 +263,11 @@
 
     lower = jnp.where(has_lower, DT, 0.0)
 
-    def select(value_of, groups, size):
-        total = jnp.zeros((groups * rows, size), F32)
-        for x in range(layers):
-            value = value_of(x)
-            high = value.astype(BF16)
-            low = (value - high.astype(F32)).astype(BF16)
-            total = total + lax.dot_general(
-                pick[pl.ds(0, groups * rows), pl.ds(x * 2 * deep, 2 * deep)],
-                jnp.concatenate([high, low], axis=1),
-                (((1,), (1,)), ((), ())),
-                preferred_element_type=F32,
-            )
-        return total
-
     for i in range(4):
-        fixed[i] = select(lambda x, i=i: coef[i, x], 1, width)
+        fixed[i] = select(pick, layers, lambda x, i=i: coef[i, x], 1)
     for c in range(2):
         near[c, pl.ds(0, rows), :] = select(
-            lambda x, c=c: eb[c, x, pl.ds(0, width), :], 1, width
+            pick, layers, lambda x, c=c: eb[c, x, pl.ds(0, width), :], 1
         )
     memory[...] = jnp.zeros_like(memory)
 
@@ -368,7 +373,7 @@
         cols = pl.ds(part_of * size, size)
         here = pl.ds(base + part_of * size, size)
         last = isinstance(n, int)
-        total = select(lambda x: buf[source, x, here, :], 1 if last else 3, size)
+        total = select(pick, layers, lambda x: buf[source, x, here, :], 1 if last else 3)
         planes[n, c, :, cols] = total[:rows, :]
         if last:
             return
@@ -395,7 +400,7 @@
             cols = pl.ds(part_of * size, size)
             for i, buf, base in ((4, eb, 0), (5, hb, PAD)):
                 here = pl.ds(base + part_of * size, size)
-                near[i, :, cols] = select(lambda x: buf[2, x, here, :], 3, size)
+                near[i, :, cols] = select(pick, layers, lambda x: buf[2, x, here, :], 3)
 
     def foresee():
         final = STEPS - 1
@@ -460,6 +465,9 @@
         peers = sum(p.astype(jnp.int32) for p in (me >= reach[i], me < count - reach[i]))
         pl.semaphore_wait(met_sem.at[i], peers)
 
+    def due(n, c):
+        return (n < STEPS - 2) | (c < CHUNKS - HELD)
+
     def send_up(n, c, slot):
         @pl.when(has_upper)
         def _():
@@ -469,9 +477,29 @@
             return
         partial_h(c * chunk, chunk)
 
-        @pl.when(has_upper)
+        @pl.when(has_upper & due(n, c))
         def _():
             send_h(c, slot).start()
+
+    to_scalars = pltpu.make_async_copy(rot, rot_s, rot_sem)
+    to_scalars.start()
+
+    def fold():
+        to_scalars.wait()
+        for c in range(4):
+
+            def body(m, carry, c=c):
+                here = pl.ds(pl.multiple_of(8 * m, 8), layers)
+                plane = [planes[n, c, here, :] for n in range(STEPS)]
+                for r in range(2):
+                    for f in range(nf):
+                        value = rot_s[r, f, c] * plane[0]
+                        for n in range(1, STEPS):
+                            value = value + rot_s[r, f, n * 4 + c] * plane[n]
+                        mon[r, c, f, m] = value
+                return carry
+
+            lax.fori_loop(0, nm, body, 0)
 
     def step(n, carry):
         last = isinstance(n, int)
@@ -494,7 +522,7 @@
 
             if not last:
 
-                @pl.when(has_lower)
+                @pl.when(has_lower & due(n, c))
                 def _(c=c):
                     send_e(c, eb, other).start()
 
@@ -530,65 +558,68 @@
         return pltpu.make_async_remote_copy(
             src_ref=part,
             dst_ref=gathered.at[slot],
-            send_sem=sp_sem.at[k],
-            recv_sem=rp_sem.at[k],
+            send_sem=sp_sem,
+            recv_sem=rp_sem,
             device_id={"gx": lax.rem(me + k, count)},
             device_id_type=MESH,
         )
 
     for k in range(1, count):
         share(k, me).start()
+    for c in range(CHUNKS - HELD, CHUNKS):
+
+        @pl.when(has_upper)
+        def _(c=c):
+            send_h(c, (STEPS - 1) % 2).start()
+
+        @pl.when(has_lower)
+        def _(c=c):
+            send_e(c, eb, (STEPS - 1) % 2).start()
+
     gathered[me] = part[...]
 
     step(STEPS - 1, 0)
-
+    fold()
+
+    others = gathered.at[pl.ds(0, count - 1)]
+    arrivals = pltpu.make_async_remote_copy(
+        src_ref=others,
+        dst_ref=others,
+        send_sem=sp_sem,
+        recv_sem=rp_sem,
+        device_id={"gx": lax.rem(me + 1, count)},
+        device_id_type=MESH,
+    )
+    arrivals.wait_send()
+    arrivals.wait_recv()
+    total = gathered[0]
     for k in range(1, count):
-        share(k, lax.rem(me - k + count, count)).wait()
-    full = gathered[0]
-    for k in range(1, count):
-        full = full + gathered[k]
+        total = total + gathered[k]
+    full[...] = total
+
+
+def place_kernel(
+    scale, eb, hb, mon, rot, full, el_out, ma_out, mon_out, inter_out, inter, sems
+):
+    width, nm = el_out.shape[2], mon.shape[3]
+    copies = [
+        pltpu.make_async_copy(eb.at[:, :, pl.ds(0, width)], el_out, sems.at[0]),
+        pltpu.make_async_copy(hb.at[:, :, pl.ds(PAD, width)], ma_out, sems.at[1]),
+        pltpu.make_async_copy(mon, mon_out, sems.at[2]),
+        pltpu.make_async_copy(inter, inter_out, sems.at[3]),
+    ]
+    for copy in copies[:3]:
+        copy.start()
     for r in range(2):
         out = lax.dot_general(
-            full,
+            full[...],
             rot[r],
             (((1,), (1,)), ((), ())),
             preferred_element_type=F32,
             precision=lax.Precision.HIGHEST,
         )
-        inter_ref[r] = scale * out[:nm, :]
-
-
-def place_kernel(
-    eb, hb, planes, rot, inter, el_out, ma_out, mon_out, inter_out, mon, rot_s, sems, mon_sem
-):
-    layers, width = el_out.shape[1:3]
-    nf, nm = mon.shape[2:4]
-    to_scalars = pltpu.make_async_copy(rot, rot_s, sems.at[3])
-    to_scalars.start()
-    copies = [
-        pltpu.make_async_copy(eb.at[:, :, pl.ds(0, width)], el_out, sems.at[0]),
-        pltpu.make_async_copy(hb.at[:, :, pl.ds(PAD, width)], ma_out, sems.at[1]),
-        pltpu.make_async_copy(inter, inter_out, sems.at[2]),
-    ]
-    for copy in copies:
-        copy.start()
-    to_scalars.wait()
-    for c in range(4):
-
-        def fold(m, carry, c=c):
-            rows = pl.ds(pl.multiple_of(8 * m, 8), layers)
-            plane = [planes[n, c, rows, :] for n in range(STEPS)]
-            for r in range(2):
-                for f in range(nf):
-                    value = rot_s[r, f, c] * plane[0]
-                    for n in range(1, STEPS):
-                        value = value + rot_s[r, f, n * 4 + c] * plane[n]
-                    mon[r, c, f, m] = value
-            return carry
-
-        lax.fori_loop(0, nm, fold, 0)
-        copies.append(pltpu.make_async_copy(mon.at[:, c], mon_out.at[:, c], mon_sem.at[c]))
-        copies[-1].start()
+        inter[r] = scale * out[:nm, :]
+    copies[3].start()
     for copy in copies:
         copy.wait()
 
@@ -617,11 +648,11 @@
     padded = (3, layers, width + PAD, deep)
     final = (field, field, (2, 4, nf, nm, layers, width), (2, nm, nf))
     planar = (8 * nm, width)
-    shapes = (padded, padded, (STEPS, 4) + planar, (2, nf, deep), (2, nm, nf))
+    shapes = (padded, padded, final[2], (2, nf, deep), (8, deep))
     kept = 4 * sum(math.prod(shape) for shape in shapes[:3]) + 2**17
     dma = pltpu.SemaphoreType.DMA
     held = pl.pallas_call(
-        functools.partial(main_kernel, count, scale),
+        functools.partial(main_kernel, count),
         out_shape=tuple(pltpu.VMEM(shape, F32) for shape in shapes),
         in_specs=[smem] * 6 + [vmem] + [hbm] * 3,
         out_specs=(vmem,) * 5,
@@ -634,6 +665,7 @@
             pltpu.VMEM((4, layers, width, deep), F32),
             pltpu.VMEM((layers, width, deep), jnp.int32),
             pltpu.VMEM((3 * 8 * nm, layers * 2 * deep), BF16),
+            pltpu.VMEM((STEPS, 4) + planar, F32),
             pltpu.VMEM((4,) + planar, F32),
             pltpu.VMEM((4,) + planar, F32),
             pltpu.VMEM((2, 2) + planar, F32),
@@ -644,13 +676,15 @@
             pltpu.VMEM((nm, 8, width), F32),
             pltpu.VMEM((8, deep), F32),
             pltpu.VMEM((count, 8, deep), F32),
+            pltpu.SMEM((2, nf, deep), F32),
+            dma,
             dma((5,)),
             dma((CHUNKS,)),
             dma((2, CHUNKS)),
             dma((CHUNKS,)),
             dma((2, CHUNKS)),
-            dma((count,)),
-            dma((count,)),
+            dma,
+            dma,
             dma((4,)),
             pltpu.SemaphoreType.REGULAR((count.bit_length(),)),
         ],
@@ -668,14 +702,12 @@
         *(pltpu.with_memory_space_constraint(a, pltpu.HBM) for a in (electric, magnetic, material)),
     )
     return pl.pallas_call(
-        place_kernel,
+        functools.partial(place_kernel, scale),
         out_shape=tuple(jax.ShapeDtypeStruct(shape, F32) for shape in final),
         in_specs=[vmem] * 5,
         out_specs=(hbm,) * 4,
         scratch_shapes=[
-            pltpu.VMEM(final[2], F32),
-            pltpu.SMEM((2, nf, deep), F32),
-            dma((4,)),
+            pltpu.VMEM(final[3], F32),
             dma((4,)),
         ],
         compiler_params=pltpu.CompilerParams(vmem_limit_bytes=16 * 2**20),

time: 48.2 us -> 46.8 us (0.971); the launches traced: 48.1 us -> 46 us
  Pallas kernels: 47.4 us -> 45.3 us
    pallas_call x2, Pallas kernels: 47.4 us -> 45.3 us  [the longest x1 43.3 us: on_device(): pl.pallas_call(functools.partial(main_kernel, count), out_shape=tuple((pl...]
where the time goes in v3:
time: 46.8 us; the launch traced here: 46 us
  Pallas kernels  45.3 us (97%)
  between operations  0.64 us (1%)
    pallas_call x1, Pallas kernels, on_device(): pl.pallas_call(functools.partial(main_kernel, count), out_shape=tuple((pl...  43.3 us
    pallas_call x1, Pallas kernels, on_device(): pl.pallas_call(functools.partial(place_kernel, scale), out_shape=tuple((j...  2.05 us

profile of v3, /device:TPU:0, one launch (start us, length us, event | category | flops | bytes accessed | tf_op | source)
XLA Modules:
  0.0 46.0 jit_solution(1051257013322275192)
XLA Ops:
  0.6 43.3 %shard_map.129 = (f32[3,4,264,128]{3,2,1,0:T(8,128)S(1)}, f32[3,4,264,128]{3,2,1,0:T(8,128)S(1)}, f32[2,4,8,4,4,256]{5,4,3,2,1,0:T(4,128)S(1)}, f32[2,8,128]{2,1,0:T(8,128)S(1)}, f32[8,128]{1,0:T(8,128)S(1)}) custom-call(f32[4]{0:T(128)} %perm_ref.1, f32[2]{0:T(128)} %freq_ref.1, f32[2]{0:T(128)} %damp_ref.1, f32[2]{0:T(128)} %strength_ref.1, f32[8]{0:T(128)} %omega_ref.1, ...), custom_call_target="tpu_custom_call" | custom-call | tf_op jit(solution)/shard_map/pallas_call | solution.py:654
  43.9 2.0 %shard_map.130 = (f32[3,4,256,128]{3,2,1,0:T(8,128)}, f32[3,4,256,128]{3,2,1,0:T(8,128)}, f32[2,4,8,4,4,256]{5,4,3,2,1,0:T(4,128)}, f32[2,4,8]{2,1,0:T(4,128)}) custom-call(f32[3,4,264,128]{3,2,1,0:T(8,128)S(1)} %get-tuple-element.9.eb, f32[3,4,264,128]{3,2,1,0:T(8,128)S(1)} %get-tuple-element.10.hb, f32[2,4,8,4,4,256]{5,4,3,2,1,0:T(4,128)S(1)} %get-tuple-element.11.mon, ...), custom_call_target="tpu_custom_call" | custom-call | tf_op jit(solution)/shard_map/pallas_call | solution.py:704

commit v4 on v3

--- a/solution.py
+++ b/solution.py
@@ -14,6 +14,7 @@
 ROWS = 32
 PAD = 8
 HELD = 3
+FOLD = 4
 MESH = pl.DeviceIdType.MESH
 VMEM_BYTES = 67043328
 F32 = jnp.float32
@@ -362,11 +363,13 @@
                 update(x, y, size, *args)
 
     def note(n, c, product):
+        while product.shape[1] > deep:
+            half = product.shape[1] // 2
+            product = product[:, :half] + product[:, half:]
         sums = jnp.sum(product.reshape(nm, 8, product.shape[1]), axis=1)
         value = jnp.sum(sums, axis=1, keepdims=True)
         here = lax.broadcasted_iota(jnp.int32, (nm, deep), 1) == n * 4 + c
-        kept = part[pl.ds(0, nm), :]
-        part[pl.ds(0, nm), :] = kept + jnp.where(here, value, 0.0)
+        return jnp.where(here, value, 0.0)
 
     def record(n, part_of, buf, base, source, c):
         size = width // 2
@@ -376,8 +379,7 @@
         total = select(pick, layers, lambda x: buf[source, x, here, :], 1 if last else 3)
         planes[n, c, :, cols] = total[:rows, :]
         if last:
-            return
-        note(n, c, total[:rows, :] * modes[c, :, cols])
+            return 0.0
         if c < 2:
             field = near[c, pl.ds(0, rows), cols]
             polar = memory[1, c, :, cols]
@@ -386,13 +388,16 @@
             memory[0, c, :, cols] = current
             memory[1, c, :, cols] = polar + DT * current
         near[c, :, cols] = total
+        return note(n, c, total[:rows, :] * modes[c, :, cols])
 
     def record_all(n, part_of):
+        noted = 0.0
         for c in range(2):
-            record(n, part_of, eb, 0, c, c)
-            record(n, part_of, hb, PAD, c, 2 + c)
+            noted = noted + record(n, part_of, eb, 0, c, c)
+            noted = noted + record(n, part_of, hb, PAD, c, 2 + c)
         if isinstance(n, int):
             return
+        part[...] += noted
 
         @pl.when(n == STEPS - 2)
         def _():
@@ -424,11 +429,13 @@
             (hz - behind(hz)) - (hy - hy_last),
             (hx - hx_last) - (hz - hz_below),
         )
+        products = [0.0] * 4
         for c, field in enumerate((ex, ey)):
             current = fixed[0] * memory[0, c] + fixed[1] * field - fixed[2] * memory[1, c]
-            note(final, c, (field + fixed[3] * (curl[c] - current)) * modes[c])
-        note(final, 2, hx * modes[2])
-        note(final, 3, hy * modes[3])
+            final_field = field + fixed[3] * (curl[c] - current)
+            products[c] = products[c] + final_field * modes[c]
+        products[2] = products[2] + hx * modes[2]
+        products[3] = products[3] + hy * modes[3]
 
         @pl.when(has_upper)
         def _():
@@ -444,11 +451,12 @@
             return jnp.where(line < 4, ref[...].reshape(rows, width), 0.0)
 
         rise = jnp.where(line == 0, pltpu.roll(hz, rows - top, 0), 0.0)
-        note(final, 1, known(from_up) * rise)
+        products[1] = products[1] + known(from_up) * rise
         step_x = (ey - behind(ey)) + (ez - ez_last)
         fall = placed([(DT * ez, 0), (-DT * step_x, 0), (DT * ey, 0)]) * known(from_down)
         for at_line, c in enumerate((3, 0, 1)):
-            note(final, c, jnp.where(line == at_line, fall, 0.0))
+            products[c] = products[c] + jnp.where(line == at_line, fall, 0.0)
+        part[...] += sum(note(final, c, products[c]) for c in range(4))
 
     reach = [d for d in (4 << i for i in range(count.bit_length())) if d < count]
 
@@ -484,18 +492,19 @@
     to_scalars = pltpu.make_async_copy(rot, rot_s, rot_sem)
     to_scalars.start()
 
-    def fold():
-        to_scalars.wait()
+    def fold(begin, end):
         for c in range(4):
 
             def body(m, carry, c=c):
                 here = pl.ds(pl.multiple_of(8 * m, 8), layers)
-                plane = [planes[n, c, here, :] for n in range(STEPS)]
+                plane = [planes[n, c, here, :] for n in range(begin, end)]
                 for r in range(2):
                     for f in range(nf):
-                        value = rot_s[r, f, c] * plane[0]
-                        for n in range(1, STEPS):
-                            value = value + rot_s[r, f, n * 4 + c] * plane[n]
+                        value = rot_s[r, f, begin * 4 + c] * plane[0]
+                        for n in range(begin + 1, end):
+                            value = value + rot_s[r, f, n * 4 + c] * plane[n - begin]
+                        if begin > 0:
+                            value = mon[r, c, f, m] + value
                         mon[r, c, f, m] = value
                 return carry
 
@@ -529,6 +538,9 @@
             if c > 0:
                 send_up(n, c - 1, other)
             sweep(update_e, range(1, top), c, slot)
+            if last and c == FOLD:
+                to_scalars.wait()
+                fold(0, STEPS - 1)
             if c == CHUNKS // 2 - 1:
                 record_all(n, 0)
         send_up(n, CHUNKS - 1, other)
@@ -579,7 +591,7 @@
     gathered[me] = part[...]
 
     step(STEPS - 1, 0)
-    fold()
+    fold(STEPS - 1, STEPS)
 
     others = gathered.at[pl.ds(0, count - 1)]
     arrivals = pltpu.make_async_remote_copy(
@@ -601,7 +613,7 @@
 def place_kernel(
     scale, eb, hb, mon, rot, full, el_out, ma_out, mon_out, inter_out, inter, sems
 ):
-    width, nm = el_out.shape[2], mon.shape[3]
+    width = el_out.shape[2]
     copies = [
         pltpu.make_async_copy(eb.at[:, :, pl.ds(0, width)], el_out, sems.at[0]),
         pltpu.make_async_copy(hb.at[:, :, pl.ds(PAD, width)], ma_out, sems.at[1]),
@@ -618,7 +630,7 @@
             preferred_element_type=F32,
             precision=lax.Precision.HIGHEST,
         )
-        inter[r] = scale * out[:nm, :]
+        inter[r] = scale * out
     copies[3].start()
     for copy in copies:
         copy.wait()
@@ -648,7 +660,7 @@
     padded = (3, layers, width + PAD, deep)
     final = (field, field, (2, 4, nf, nm, layers, width), (2, nm, nf))
     planar = (8 * nm, width)
-    shapes = (padded, padded, final[2], (2, nf, deep), (8, deep))
+    shapes = (padded, padded, final[2], (2, nf, deep), (nm, deep))
     kept = 4 * sum(math.prod(shape) for shape in shapes[:3]) + 2**17
     dma = pltpu.SemaphoreType.DMA
     held = pl.pallas_call(
@@ -674,8 +686,8 @@
             pltpu.VMEM((nm, 8, width), F32),
             pltpu.VMEM((nm, 8, width), F32),
             pltpu.VMEM((nm, 8, width), F32),
-            pltpu.VMEM((8, deep), F32),
-            pltpu.VMEM((count, 8, deep), F32),
+            pltpu.VMEM((nm, deep), F32),
+            pltpu.VMEM((count, nm, deep), F32),
             pltpu.SMEM((2, nf, deep), F32),
             dma,
             dma((5,)),

time: 46.8 us -> 46 us (0.983); the launches traced: 46 us -> 45.8 us
  no operation moved by 1% of the time
where the time goes in v4:
time: 46 us; the launch traced here: 45.8 us
  Pallas kernels  45.2 us (98%)
  between operations  0.64 us (1%)
    pallas_call x1, Pallas kernels, on_device(): pl.pallas_call(functools.partial(main_kernel, count), out_shape=tuple((pl...  43.1 us
    pallas_call x1, Pallas kernels, on_device(): pl.pallas_call(functools.partial(place_kernel, scale), out_shape=tuple((j...  2.05 us

profile of v4, /device:TPU:0, one launch (start us, length us, event | category | flops | bytes accessed | tf_op | source)
XLA Modules:
  0.0 45.8 jit_solution(15816955115325298873)
XLA Ops:
  0.6 43.1 %shard_map.129 = (f32[3,4,264,128]{3,2,1,0:T(8,128)S(1)}, f32[3,4,264,128]{3,2,1,0:T(8,128)S(1)}, f32[2,4,8,4,4,256]{5,4,3,2,1,0:T(4,128)S(1)}, f32[2,8,128]{2,1,0:T(8,128)S(1)}, f32[4,128]{1,0:T(4,128)S(1)}) custom-call(f32[4]{0:T(128)} %perm_ref.1, f32[2]{0:T(128)} %freq_ref.1, f32[2]{0:T(128)} %damp_ref.1, f32[2]{0:T(128)} %strength_ref.1, f32[8]{0:T(128)} %omega_ref.1, ...), custom_call_target="tpu_custom_call" | custom-call | tf_op jit(solution)/shard_map/pallas_call | solution.py:666
  43.8 2.0 %shard_map.130 = (f32[3,4,256,128]{3,2,1,0:T(8,128)}, f32[3,4,256,128]{3,2,1,0:T(8,128)}, f32[2,4,8,4,4,256]{5,4,3,2,1,0:T(4,128)}, f32[2,4,8]{2,1,0:T(4,128)}) custom-call(f32[3,4,264,128]{3,2,1,0:T(8,128)S(1)} %get-tuple-element.9.eb, f32[3,4,264,128]{3,2,1,0:T(8,128)S(1)} %get-tuple-element.10.hb, f32[2,4,8,4,4,256]{5,4,3,2,1,0:T(4,128)S(1)} %get-tuple-element.11.mon, ...), custom_call_target="tpu_custom_call" | custom-call | tf_op jit(solution)/shard_map/pallas_call | solution.py:716
